TPU v7x, 32 devices: a whole 2x2x4 slice. The times are simulated.
32 devices in a mesh: groups: 2 (over x), ep: 16 (over z, y, core).
Axes of the slice: x: 2, y: 2, z: 4, core: 2. Of those that a mesh axis runs over, the one named last changes fastest.
Arguments:
- states: float32 [2, 256, 2048], P(None, ('groups', 'ep')), parts along dimension 1, may hold values from -6 to 6
- attn_gain: float32 [2048], replicated, may hold values from 0.1 to 1.9
- moe_gain: float32 [2048], replicated, may hold values from 0.1 to 1.9
- w_query: bfloat16 [2048, 2048], P(None, 'ep'), may hold values from -11 to 11
- w_key: bfloat16 [2048, 256], P(None, 'ep'), may hold values from -0.125 to 0.125
- w_value: bfloat16 [2048, 256], P(None, 'ep'), may hold values from -0.125 to 0.125
- w_output: bfloat16 [2048, 2048], P('ep'), may hold values from -0.125 to 0.125
- w_gate_up: bfloat16 [16, 2048, 1536], P('ep'), may hold values from -0.125 to 0.125
- w_down: bfloat16 [16, 768, 2048], P('ep'), may hold values from -0.21875 to 0.21875
- key_cache: bfloat16 [64, 1024, 256], P(('groups', 'ep')), parts along dimension 0, may hold values from -60 to 60
- value_cache: bfloat16 [64, 1024, 256], P(('groups', 'ep')), parts along dimension 0, may hold values from -24 to 24
- cache_lengths: int32 [64], P(('groups', 'ep')), parts along dimension 0, may hold values from 1 to 1024, as said below
- prefix_slot: int32 [256], P(('groups', 'ep')), parts along dimension 0, may hold values from 0 to 1
- routes: int32 [256, 2, 8], P(('groups', 'ep')), parts along dimension 0, may hold values from 0 to 15, all different within a row; in each aligned block of 16 rows (0 to 15, 16 to 31, ..., all dimensions but the last counted through in order) at most 16 rows name the same one
- gate_weights: float32 [2, 256, 8], P(None, ('groups', 'ep')), parts along dimension 1, may hold values from 0.05 to 0.5
Outputs:
- layer_out: float32 [2, 256, 2048], P(None, ('groups', 'ep')), parts along dimension 1
- appended_kv: bfloat16 [2, 256, 512], P(None, ('groups', 'ep')), parts along dimension 1
There are 2 independent parts, one for each index of `groups`. A program takes and returns all parts, laid end to end along the dimension named above; an argument that names none is the same for every part. Nothing has to cross between parts.
Inputs may be any that keep to these rules, and one draw needn't show every extreme that they name: `cache_lengths`: positions beyond a prefix's length are unused; some prefix is full at 1024. `routes`: over both steps together, the 8 branches of one ep device choose any one expert at most 16 times; a branch's 8 experts at one step differ.
All inputs are finite; a program needn't handle non-finite values.
Results may differ from a plain program's by a relative error of at most 0.0024.
The roundings to bfloat16 on the way count: a program that leaves them out, or rounds other values in their place, can miss the bound.
Values may be sent and summed in bfloat16 or wider, within the bound.
A program may use at most 128 MiB of HBM per device.

v0:
```python
import math
import jax
import jax.numpy as jnp
from jax import lax
from jax.sharding import PartitionSpec as P

HQ = 16
KVH = 2
HD = 128
TOPK = 8
EPS = 1e-06
THETA = 1000000.0


def rms_scale(values, gain):
    squares = jnp.mean(values * values, axis=-1, keepdims=True)
    return values * lax.rsqrt(squares + EPS) * gain


def rotate(vectors, positions):
    head_size = vectors.shape[-1]
    half_size = head_size // 2
    inverse_rate = THETA ** (-(jnp.arange(half_size).astype(jnp.float32) * 2.0 / head_size))
    phases = positions[..., None, None] * inverse_rate
    cosine = jnp.cos(phases)
    sine_part = jnp.sin(phases)
    first_half = vectors[..., :half_size]
    second_half = vectors[..., half_size:]
    return jnp.concatenate(
        [
            first_half * cosine - second_half * sine_part,
            second_half * cosine + first_half * sine_part,
        ],
        axis=-1,
    )


def attend_block(queries, new_keys, new_values, key_block, value_block, lengths, slots):
    step_count, row_count, head_count, head_size = queries.shape
    prefix_count, cache_span, kv_heads, _ = key_block.shape
    group_size = head_count // kv_heads
    grouped = queries.reshape(step_count, row_count, kv_heads, group_size, head_size)
    inv_root = 1.0 / math.sqrt(head_size)
    far_scores = (
        jnp.einsum("srkgd,pckd->srkgpc", grouped, key_block, preferred_element_type=jnp.float32)
        * inv_root
    )
    visible = (jnp.arange(cache_span)[None, None, :] < lengths[None, :, None]) & (
        slots[:, None, None] == jnp.arange(prefix_count)[None, :, None]
    )
    far_scores = jnp.where(visible[None, :, None, None], far_scores, -1e30)
    own_scores = (
        jnp.einsum("srkgd,trkd->srkgt", grouped, new_keys, preferred_element_type=jnp.float32)
        * inv_root
    )
    causal = jnp.arange(step_count)[None, :] <= jnp.arange(step_count)[:, None]
    own_scores = jnp.where(causal[:, None, None, None, :], own_scores, -1e30)
    peak = jnp.maximum(jnp.max(far_scores, axis=(-2, -1)), jnp.max(own_scores, axis=-1))
    far_weights = jnp.exp(far_scores - peak[..., None, None])
    own_weights = jnp.exp(own_scores - peak[..., None])
    normalizer = jnp.sum(far_weights, axis=(-2, -1)) + jnp.sum(own_weights, axis=-1)
    far_probs = (far_weights / normalizer[..., None, None]).astype(jnp.bfloat16)
    own_probs = (own_weights / normalizer[..., None]).astype(jnp.bfloat16)
    attended = jnp.einsum(
        "srkgpc,pckd->srkgd", far_probs, value_block, preferred_element_type=jnp.float32
    )
    attended = attended + jnp.einsum(
        "srkgt,trkd->srkgd", own_probs, new_values, preferred_element_type=jnp.float32
    )
    return attended.reshape(step_count, row_count, head_count * head_size).astype(jnp.bfloat16)


def shards(
    states,
    attn_gain,
    moe_gain,
    w_query,
    w_key,
    w_value,
    w_output,
    w_gate_up,
    w_down,
    key_cache,
    value_cache,
    cache_lengths,
    prefix_slot,
    routes,
    gate_weights,
):
    devices = lax.axis_size("ep")
    step_count, row_count, model_width = states.shape
    query_cols = w_query.shape[1]
    kv_cols = w_key.shape[1]
    normed = rms_scale(states, attn_gain).astype(jnp.bfloat16)
    joined = jnp.concatenate([w_query, w_key, w_value], axis=1)
    head_parts = jnp.einsum(
        "srd,dc->src",
        lax.all_gather(normed, "ep", axis=1, tiled=True),
        joined,
        preferred_element_type=jnp.float32,
    )
    own_cols = lax.all_to_all(head_parts, "ep", split_axis=1, concat_axis=2, tiled=True)
    own_cols = own_cols.reshape(step_count, row_count, devices, query_cols + 2 * kv_cols)
    queries = own_cols[..., :query_cols].reshape(step_count, row_count, HQ, HD)
    new_keys = own_cols[..., query_cols : query_cols + kv_cols].reshape(
        step_count, row_count, KVH, HD
    )
    new_values = (
        own_cols[..., query_cols + kv_cols :]
        .reshape(step_count, row_count, KVH, HD)
        .astype(jnp.bfloat16)
    )
    prefix_count, cache_span, _ = key_cache.shape
    lengths_here = jnp.sum(
        jnp.where(
            prefix_slot[:, None] == jnp.arange(prefix_count)[None, :], cache_lengths[None, :], 0
        ),
        axis=1,
    )
    positions = (
        lengths_here.astype(jnp.float32)[None, :]
        + jnp.arange(step_count).astype(jnp.float32)[:, None]
    )
    queries = rotate(queries, positions).astype(jnp.bfloat16)
    new_keys = rotate(new_keys, positions).astype(jnp.bfloat16)
    attended = attend_block(
        queries,
        new_keys,
        new_values,
        key_cache.reshape(prefix_count, cache_span, KVH, HD),
        value_cache.reshape(prefix_count, cache_span, KVH, HD),
        cache_lengths,
        prefix_slot,
    )
    w_columns = lax.all_to_all(w_output, "ep", split_axis=1, concat_axis=0, tiled=True)
    column_part = jnp.einsum(
        "srf,fc->src",
        lax.all_gather(attended, "ep", axis=1, tiled=True),
        w_columns,
        preferred_element_type=jnp.float32,
    )
    projected = lax.all_to_all(column_part, "ep", split_axis=1, concat_axis=2, tiled=True)
    hidden = states + projected
    moe_input = (
        rms_scale(hidden, moe_gain)
        .astype(jnp.bfloat16)
        .reshape(step_count * row_count, model_width)
    )
    expert_count = w_gate_up.shape[0] * devices
    capacity = max(2, 4 * row_count * TOPK // expert_count)
    flat_routes = jnp.swapaxes(routes, 0, 1).reshape(-1)
    onehot = (flat_routes[:, None] == jnp.arange(expert_count)[None, :]).astype(jnp.int32)
    running = jnp.cumsum(onehot, axis=0) - 1
    within = jnp.sum(onehot * running, axis=1)
    slot_index = flat_routes * capacity + within
    dispatch = (jnp.arange(expert_count * capacity)[:, None] == slot_index[None, :]).astype(
        jnp.bfloat16
    )
    repeated = jnp.repeat(moe_input, TOPK, axis=0)
    outgoing = jnp.dot(dispatch, repeated, preferred_element_type=jnp.float32).astype(jnp.bfloat16)
    outgoing = outgoing.reshape(expert_count, capacity, model_width)
    both = jnp.einsum(
        "nsd,df->nsf",
        lax.all_to_all(outgoing, "ep", split_axis=0, concat_axis=0, tiled=True),
        w_gate_up[0],
        preferred_element_type=jnp.float32,
    )
    half_cols = both.shape[-1] // 2
    activation = (jax.nn.silu(both[..., :half_cols]) * both[..., half_cols:]).astype(jnp.bfloat16)
    expert_done = jnp.einsum(
        "nsf,fd->nsd", activation, w_down[0], preferred_element_type=jnp.float32
    ).astype(jnp.bfloat16)
    returned = lax.all_to_all(expert_done, "ep", split_axis=0, concat_axis=0, tiled=True)
    picked = returned.reshape(expert_count * capacity, model_width)[slot_index]
    picked = picked.astype(jnp.float32).reshape(step_count, row_count, TOPK, model_width)
    mixture = jnp.sum(gate_weights[..., None] * picked, axis=2)
    appended = jnp.concatenate(
        [
            new_keys.reshape(step_count, row_count, KVH * HD),
            new_values.reshape(step_count, row_count, KVH * HD),
        ],
        axis=-1,
    )
    return (hidden + mixture, appended)


def solution(mesh):
    return jax.shard_map(
        shards,
        mesh=mesh,
        in_specs=(
            P(None, ("groups", "ep"), None),
            P(),
            P(),
            P(None, "ep"),
            P(None, "ep"),
            P(None, "ep"),
            P("ep", None),
            P("ep", None, None),
            P("ep", None, None),
            P(("groups", "ep"), None, None),
            P(("groups", "ep"), None, None),
            P(("groups", "ep")),
            P(("groups", "ep")),
            P(("groups", "ep"), None, None),
            P(None, ("groups", "ep"), None),
        ),
        out_specs=(P(None, ("groups", "ep"), None), P(None, ("groups", "ep"), None)),
        check_vma=False,
    )
```

profile of v0, /device:TPU:9, one launch (start us, length us, event | category | flops | bytes accessed | tf_op | source)
XLA Modules:
  0.0 204.8 jit_solution(11933007128233373446)
XLA Ops:
  7.2 1.2 multiply_reduce_fusion.1
  8.4 1.6 multiply_convert_fusion.1
  10.0 2.0 copy.137
  13.2 2.2 %reshape.240 = bf16[2,1024,2,128]{3,2,1,0:T(2,128)(2,1)} reshape(bf16[2,1024,256]{2,1,0:T(8,128)(2,1)} %param.24) | data formatting | bytes 2097152 | tf_op jit(solution)/shard_map/reshape | solution.py:130
  15.5 2.1 %reshape.242 = bf16[2,1024,2,128]{3,2,1,0:T(2,128)(2,1)} reshape(bf16[2,1024,256]{2,1,0:T(8,128)(2,1)} %param.25) | data formatting | bytes 2097152 | tf_op jit(solution)/shard_map/reshape | solution.py:131
  17.8 31.6 %all-gather.3.cloned.1.call-done = bf16[2,128,2048]{2,1,0:T(8,128)(2,1)} async-done(((bf16[2,8,2048]{2,1,0:T(8,128)(2,1)}), bf16[2,128,2048]{2,1,0:T(8,128)(2,1)}) %all-gather.3.cloned.1.call-update) | async-done | bytes 1048592 | tf_op jit(solution)/shard_map/all_gather | solution.py:98
  49.4 1.9 fusion.19
  52.1 4.9 %all-to-all-start = ((f32[2,128,160]{2,0,1:T(2,128)}), f32[2,128,160]{2,0,1:T(2,128)S(1)}, u32[]{:S(2)}, u32[]{:S(2)}) async-start(f32[2,128,160]{2,0,1:T(2,128)} %copy.138), calls=%async_computation | async-start | bytes 524288 | tf_op jit(solution)/shard_map/all_to_all | solution.py:102
  57.7 8.0 %all-to-all-done = f32[2,128,160]{2,0,1:T(2,128)S(1)} async-done(((f32[2,128,160]{2,0,1:T(2,128)}), f32[2,128,160]{2,0,1:T(2,128)S(1)}, u32[]{:S(2)}, u32[]{:S(2)}) %all-to-all-start) | async-done | bytes 163872 | tf_op jit(solution)/shard_map/all_to_all | solution.py:102
  67.5 2.0 bitcast_reduce_fusion
  72.3 2.0 copy_bitcast_fusion
  74.3 5.5 %all-to-all-start.1 = ((bf16[128,16,128]{2,0,1:T(8,128)(2,1)}), bf16[128,16,128]{2,0,1:T(8,128)(2,1)}, u32[]{:S(2)}, u32[]{:S(2)}) async-start(bf16[128,16,128]{2,0,1:T(8,128)(2,1)} %copy_bitcast_fusion), calls=%async_computation.1 | async-start | bytes 1048576 | tf_op jit(solution)/shard_map/all_to_all | solution.py:135
  80.7 15.2 %all-to-all-done.1 = bf16[128,16,128]{2,0,1:T(8,128)(2,1)} async-done(((bf16[128,16,128]{2,0,1:T(8,128)(2,1)}), bf16[128,16,128]{2,0,1:T(8,128)(2,1)}, u32[]{:S(2)}, u32[]{:S(2)}) %all-to-all-start.1) | async-done | bytes 524320 | tf_op jit(solution)/shard_map/all_to_all | solution.py:135
  95.9 15.3 %all-gather.5.cloned.1.call-done = bf16[2,128,2048]{2,1,0:T(8,128)(2,1)} async-done(((bf16[2,8,2048]{2,1,0:T(8,128)(2,1)}), bf16[2,128,2048]{2,1,0:T(8,128)(2,1)}) %all-gather.5.cloned.1.call-update) | async-done | bytes 1048592 | tf_op jit(solution)/shard_map/all_gather | solution.py:138
  111.3 1.8 fusion.45
  113.8 4.9 %all-to-all-start.2 = ((f32[2,128,128]{2,0,1:T(2,128)}), f32[2,128,128]{2,0,1:T(2,128)S(1)}, u32[]{:S(2)}, u32[]{:S(2)}) async-start(f32[2,128,128]{2,0,1:T(2,128)} %copy.161), calls=%async_computation.2 | async-start | bytes 262144 | tf_op jit(solution)/shard_map/all_to_all | solution.py:142
  120.7 3.9 %all-to-all-done.2 = f32[2,128,128]{2,0,1:T(2,128)S(1)} async-done(((f32[2,128,128]{2,0,1:T(2,128)}), f32[2,128,128]{2,0,1:T(2,128)S(1)}, u32[]{:S(2)}, u32[]{:S(2)}) %all-to-all-start.2) | async-done | bytes 131104 | tf_op jit(solution)/shard_map/all_to_all | solution.py:142
  126.0 30.0 %all_to_all.62 = bf16[16,16,2048]{2,1,0:T(8,128)(2,1)S(1)} all-to-all(bf16[16,16,2048]{2,1,0:T(8,128)(2,1)S(1)} %bitcast.120), channel_id=1, replica_groups=mesh['groups'=2,'ep'=16] {'ep'}, dimensions={0} | all-to-all | bytes 2097152 | tf_op jit(solution)/shard_map/all_to_all | solution.py:164
  156.0 4.6 %fusion = f32[16,16,1536]{2,1,0:T(8,128)S(1)} fusion(bf16[16,16,2048]{2,1,0:T(8,128)(2,1)S(1)} %all_to_all.62, bf16[1,2048,1536]{2,1,0:T(8,128)(2,1)} %param.22), kind=kOutput, calls=%fused_computation.1 | convolution fusion | flops 1610612736 | bytes 8912896 | tf_op jit(solution)/shard_map/nsd,df->nsf/dot_general | solution.py:162
  160.6 2.1 %fusion.4 = bf16[16,16,2048]{2,1,0:T(8,128)(2,1)} fusion(bf16[1,768,2048]{2,1,0:T(8,128)(2,1)S(1)} %copy-done, f32[16,16,1536]{2,1,0:T(8,128)S(1)} %fusion), kind=kOutput, calls=%fused_computation.6 | convolution fusion | flops 807010304 | bytes 5767168 | tf_op jit(solution)/shard_map/nsf,fd->nsd/dot_general | solution.py:170
  162.6 4.5 %all-to-all-start.4 = ((bf16[16,16,2048]{2,1,0:T(8,128)(2,1)}), bf16[16,16,2048]{2,1,0:T(8,128)(2,1)}, u32[]{:S(2)}, u32[]{:S(2)}) async-start(bf16[16,16,2048]{2,1,0:T(8,128)(2,1)} %fusion.4), calls=%async_computation.4 | async-start | bytes 2097152 | tf_op jit(solution)/shard_map/all_to_all | solution.py:173
  168.0 24.1 %all-to-all-done.4 = bf16[16,16,2048]{2,1,0:T(8,128)(2,1)} async-done(((bf16[16,16,2048]{2,1,0:T(8,128)(2,1)}), bf16[16,16,2048]{2,1,0:T(8,128)(2,1)}, u32[]{:S(2)}, u32[]{:S(2)}) %all-to-all-start.4) | async-done | bytes 1048608 | tf_op jit(solution)/shard_map/all_to_all | solution.py:173
  192.1 3.6 %gather_fusion = bf16[128,2048]{1,0:T(8,128)(2,1)} fusion(bf16[256,2048]{1,0:T(8,128)(2,1)} %bitcast.33, s32[1024]{0:T(1024)S(1)} %pad_clamp_fusion), kind=kCustom, calls=%fused_computation | custom fusion | bytes 1049088 | tf_op jit(solution)/shard_map/gather | solution.py:174
  195.7 1.5 fusion.13
  (85 shorter events, 13.6 us)
Async XLA Ops:
  7.2 153.4 %copy-start = (bf16[1,768,2048]{2,1,0:T(8,128)(2,1)S(1)}, bf16[1,768,2048]{2,1,0:T(8,128)(2,1)}, u32[]{:S(2)}) copy-start(bf16[1,768,2048]{2,1,0:T(8,128)(2,1)} %param.23) | copy-start | bytes 9437188
  7.2 42.2 %all-gather.3.cloned.1.call-start = ((), (), s32[]{:S(2)}) async-start(), calls=%async_computation.5 | async-start | bytes 1114112 | tf_op jit(solution)/shard_map/all_gather | solution.py:98
  13.2 4.4 %copy-start.11 = (s32[8]{0:T(128)S(1)}, s32[8]{0:T(128)}, u32[]{:S(2)}) copy-start(s32[8]{0:T(128)} %param.27) | copy-start | bytes 100
  13.2 4.5 %copy-start.8 = (s32[2]{0:T(128)S(1)}, s32[2]{0:T(128)}, u32[]{:S(2)}) copy-start(s32[2]{0:T(128)} %param.26) | copy-start | bytes 28
  13.2 36.2 %copy-start.9 = (bf16[2048,16]{0,1:T(8,128)(2,1)S(1)}, bf16[2048,16]{0,1:T(8,128)(2,1)}, u32[]{:S(2)}) copy-start(bf16[2048,16]{0,1:T(8,128)(2,1)} %param.20) | copy-start | bytes 196612
  13.2 36.2 %copy-start.10 = (bf16[2048,16]{0,1:T(8,128)(2,1)S(1)}, bf16[2048,16]{0,1:T(8,128)(2,1)}, u32[]{:S(2)}) copy-start(bf16[2048,16]{0,1:T(8,128)(2,1)} %param.19) | copy-start | bytes 196612
  52.1 13.6 %all-to-all-start = ((f32[2,128,160]{2,0,1:T(2,128)}), f32[2,128,160]{2,0,1:T(2,128)S(1)}, u32[]{:S(2)}, u32[]{:S(2)}) async-start(f32[2,128,160]{2,0,1:T(2,128)} %copy.138), calls=%async_computation | async-start | bytes 524288 | tf_op jit(solution)/shard_map/all_to_all | solution.py:102
  57.0 54.2 %all-gather.5.cloned.1.call-start = ((), (), s32[]{:S(2)}) async-start(), calls=%async_computation.6 | async-start | bytes 1114112 | tf_op jit(solution)/shard_map/all_gather | solution.py:138
  67.5 2.8 %copy-start.2 = (bf16[2,1024,2,128]{3,2,1,0:T(2,128)(2,1)S(1)}, bf16[2,1024,2,128]{3,2,1,0:T(2,128)(2,1)}, u32[]{:S(2)}) copy-start(bf16[2,1024,2,128]{3,2,1,0:T(2,128)(2,1)} %reshape.242) | copy-start | bytes 3145732
  71.2 8.6 %copy-start.3 = (s32[8,2,8]{2,1,0:T(2,128)S(1)}, s32[8,2,8]{2,1,0:T(2,128)}, u32[]{:S(2)}) copy-start(s32[8,2,8]{2,1,0:T(2,128)} %param.28) | copy-start | bytes 1540
  72.3 52.3 %copy-start.1 = (f32[2,8,2048]{2,1,0:T(8,128)S(1)}, f32[2,8,2048]{2,1,0:T(8,128)}, u32[]{:S(2)}) copy-start(f32[2,8,2048]{2,1,0:T(8,128)} %param.15) | copy-start | bytes 393220
  74.3 21.6 %all-to-all-start.1 = ((bf16[128,16,128]{2,0,1:T(8,128)(2,1)}), bf16[128,16,128]{2,0,1:T(8,128)(2,1)}, u32[]{:S(2)}, u32[]{:S(2)}) async-start(bf16[128,16,128]{2,0,1:T(8,128)(2,1)} %copy_bitcast_fusion), calls=%async_computation.1 | async-start | bytes 1048576 | tf_op jit(solution)/shard_map/all_to_all | solution.py:135
  79.9 0.5 copy-start.5
  113.8 10.8 %all-to-all-start.2 = ((f32[2,128,128]{2,0,1:T(2,128)}), f32[2,128,128]{2,0,1:T(2,128)S(1)}, u32[]{:S(2)}, u32[]{:S(2)}) async-start(f32[2,128,128]{2,0,1:T(2,128)} %copy.161), calls=%async_computation.2 | async-start | bytes 262144 | tf_op jit(solution)/shard_map/all_to_all | solution.py:142
  119.6 0.5 copy-start.6
  162.6 4.6 %copy-start.7 = (s32[128]{0:T(128)S(1)}, s32[128]{0:T(128)}, u32[]{:S(2)}) copy-start(s32[128]{0:T(128)} %copy-done.6) | copy-start | bytes 1540
  162.6 29.5 %all-to-all-start.4 = ((bf16[16,16,2048]{2,1,0:T(8,128)(2,1)}), bf16[16,16,2048]{2,1,0:T(8,128)(2,1)}, u32[]{:S(2)}, u32[]{:S(2)}) async-start(bf16[16,16,2048]{2,1,0:T(8,128)(2,1)} %fusion.4), calls=%async_computation.4 | async-start | bytes 2097152 | tf_op jit(solution)/shard_map/all_to_all | solution.py:173
  192.1 3.6 %copy-start.4 = (f32[2,8,8]{2,1,0:T(8,128)S(1)}, f32[2,8,8]{2,1,0:T(8,128)}, u32[]{:S(2)}) copy-start(f32[2,8,8]{2,1,0:T(8,128)} %param.29) | copy-start | bytes 1540
Sparse Core Ops, SparseCore 0:
  10.8 38.5 all-gather.2
  72.4 38.7 all-gather.4
where the time goes:
time: 206 us; the launch traced here: 205 us
  waiting for transfers between devices  98.3 us (48%)
  blocking collectives  30 us (15%)
  starting transfers between devices  19.9 us (10%)
  local copies, waits for them, and re-layouts  16.2 us (8%)
  matrix products  15 us (7%)
  between operations  14.4 us (7%)
  other arithmetic  11 us (5%)
    all_gather x1, waiting for transfers between devices, shards(): lax.all_gather(normed, 'ep', axis=1, tiled=True)  31.6 us
    all_to_all x1, blocking collectives, shards(): lax.all_to_all(outgoing, 'ep', split_axis=0, concat_axis=0, tiled=True)  30 us
    all_to_all x1, waiting for transfers between devices, shards(): lax.all_to_all(expert_done, 'ep', split_axis=0, concat_axis=0, tiled=True)  24.1 us
    all_gather x1, waiting for transfers between devices, shards(): lax.all_gather(attended, 'ep', axis=1, tiled=True)  15.3 us
    all_to_all x1, waiting for transfers between devices, shards(): lax.all_to_all(w_output, 'ep', split_axis=1, concat_axis=0, tiled=True)  15.2 us
    all_to_all x1, waiting for transfers between devices, shards(): lax.all_to_all(head_parts, 'ep', split_axis=1, concat_axis=2, tiled=True)  8.01 us
    all_to_all x1, starting transfers between devices, shards(): lax.all_to_all(w_output, 'ep', split_axis=1, concat_axis=0, tiled=True)  5.47 us
    all_to_all x1, starting transfers between devices, shards(): lax.all_to_all(column_part, 'ep', split_axis=1, concat_axis=2, tiled=True)  4.92 us
  transfers between devices with their start and end apart: 6, of which 6 were waited for; matrix products, arithmetic and copies ran while one was open for 6% of the time, Pallas kernels for 0%

commit v1 on v0

--- a/solution.py
+++ b/solution.py
@@ -1,3 +1,4 @@
+import functools
 import math
 import jax
 import jax.numpy as jnp
@@ -10,6 +11,35 @@
 TOPK = 8
 EPS = 1e-06
 THETA = 1000000.0
+
+
+def _render_sample(inp, d0):
+    arr_next = lax.axis_size("ep")
+    small, w2, taken_in = (arr_next, lax.axis_index("ep"), inp.shape[d0])
+    rows = [u * small if k0 == d0 else u for k0, u in enumerate(inp.shape)]
+    ready = jnp.zeros(rows, inp.dtype)
+    b_next = lax.dynamic_update_slice_in_dim(ready, inp, w2 * taken_in, axis=d0)
+    tall = mid_arr = inp
+    idx = 1
+    while idx < small // 2 + 1:
+        tall = lax.ppermute(
+            tall, axis_name="ep", perm=[(k0, (k0 + 1) % small) for k0 in range(small)]
+        )
+        b_next = lax.dynamic_update_slice_in_dim(
+            b_next, tall, (w2 - idx) % small * taken_in, axis=d0
+        )
+        if 2 * idx < small:
+            mid_arr = lax.ppermute(
+                mid_arr, axis_name="ep", perm=[(k0, (k0 - 1) % small) for k0 in range(small)]
+            )
+            b_next = lax.dynamic_update_slice_in_dim(
+                b_next, mid_arr, (w2 + idx) % small * taken_in, axis=d0
+            )
+        idx = idx + 1
+    return b_next
+
+
+blocks_render = functools.partial(_render_sample, d0=1)
 
 
 def rms_scale(values, gain):
@@ -134,10 +164,7 @@
     )
     w_columns = lax.all_to_all(w_output, "ep", split_axis=1, concat_axis=0, tiled=True)
     column_part = jnp.einsum(
-        "srf,fc->src",
-        lax.all_gather(attended, "ep", axis=1, tiled=True),
-        w_columns,
-        preferred_element_type=jnp.float32,
+        "srf,fc->src", blocks_render(attended), w_columns, preferred_element_type=jnp.float32
     )
     projected = lax.all_to_all(column_part, "ep", split_axis=1, concat_axis=2, tiled=True)
     hidden = states + projected

time: 206 us -> 225 us (1.092)
  starting transfers between devices: 19.9 us -> 51.4 us
  waiting for transfers between devices: 98.3 us -> 72.4 us
  local copies, waits for them, and re-layouts: 16.2 us -> 27.5 us
    all_to_all x1, starting transfers between devices: 4.92 us -> 21.3 us  [shards(): lax.all_to_all(column_part, 'ep', split_axis=1, concat_axis=2, tiled=True)]
    all_gather x1 -> x0, waiting for transfers between devices: 15.3 us -> none  [shards(): lax.all_gather(attended, 'ep', axis=1, tiled=True)]
    all_to_all x1, waiting for transfers between devices: 15.2 us -> 0.01 us  [shards(): lax.all_to_all(w_output, 'ep', split_axis=1, concat_axis=0, tiled=True)]
    ppermute x0 -> x15, starting transfers between devices: none -> 15.2 us  [the longest x8 10.7 us: _render_sample(): lax.ppermute(tall, axis_name='ep', perm=[(k0, (k0 + 1) % small) for k0 in...]
    dynamic_update_slice x0 -> x16, local copies, waits for them, and re-layouts: none -> 10.1 us  [the longest x8 5.03 us: _render_sample(): lax.dynamic_update_slice_in_dim(b_next, tall, (w2 - idx) % small * taken_...]
    ppermute x0 -> x15, waiting for transfers between devices: none -> 7.91 us  [the longest x7 5.6 us: _render_sample(): lax.ppermute(mid_arr, axis_name='ep', perm=[(k0, (k0 - 1) % small) for k0...]
  transfers between devices with their start and end apart: 6 -> 20, of which waited for: 6 -> 11; matrix products, arithmetic and copies ran while one was open for 6% -> 15% of each run, Pallas kernels for 0% -> 0%
where the time goes in v1:
time: 225 us; the launch traced here: 224 us
  waiting for transfers between devices  72.4 us (32%)
  starting transfers between devices  51.4 us (23%)
  blocking collectives  30 us (13%)
  local copies, waits for them, and re-layouts  27.5 us (12%)
  matrix products  16.5 us (7%)
  between operations  14.7 us (7%)
  other arithmetic  11.8 us (5%)
    all_gather x1, waiting for transfers between devices, shards(): lax.all_gather(normed, 'ep', axis=1, tiled=True)  30.3 us
    all_to_all x1, blocking collectives, shards(): lax.all_to_all(outgoing, 'ep', split_axis=0, concat_axis=0, tiled=True)  30 us
    all_to_all x1, waiting for transfers between devices, shards(): lax.all_to_all(expert_done, 'ep', split_axis=0, concat_axis=0, tiled=True)  24.1 us
    all_to_all x1, starting transfers between devices, shards(): lax.all_to_all(column_part, 'ep', split_axis=1, concat_axis=2, tiled=True)  21.3 us
    ppermute x8, starting transfers between devices, _render_sample(): lax.ppermute(tall, axis_name='ep', perm=[(k0, (k0 + 1) % small) for k0 in...  10.7 us
    all_to_all x1, waiting for transfers between devices, shards(): lax.all_to_all(head_parts, 'ep', split_axis=1, concat_axis=2, tiled=True)  6.19 us
    ppermute x7, waiting for transfers between devices, _render_sample(): lax.ppermute(mid_arr, axis_name='ep', perm=[(k0, (k0 - 1) % small) for k0...  5.6 us
    all_to_all x1, starting transfers between devices, shards(): lax.all_to_all(w_output, 'ep', split_axis=1, concat_axis=0, tiled=True)  5.46 us
  transfers between devices with their start and end apart: 20, of which 11 were waited for; matrix products, arithmetic and copies ran while one was open for 15% of the time, Pallas kernels for 0%

profile of v1, /device:TPU:9, one launch (start us, length us, event | category | flops | bytes accessed | tf_op | source)
XLA Modules:
  0.0 224.3 jit_solution(5724512397287458338)
XLA Ops:
  10.3 2.1 copy.137
  14.0 2.2 reshape.240
  16.3 2.1 reshape.242
  19.1 30.3 %all-gather.2.cloned.1.call-done = bf16[2,128,2048]{2,1,0:T(8,128)(2,1)} async-done(((bf16[2,8,2048]{2,1,0:T(8,128)(2,1)}), bf16[2,128,2048]{2,1,0:T(8,128)(2,1)}) %all-gather.2.cloned.1.call-update) | async-done | bytes 1048592 | tf_op jit(solution)/shard_map/all_gather | solution.py:128
  49.4 1.9 fusion.19
  52.1 4.9 %all-to-all-start = ((f32[2,128,160]{2,0,1:T(2,128)}), f32[2,128,160]{2,0,1:T(2,128)S(1)}, u32[]{:S(2)}, u32[]{:S(2)}) async-start(f32[2,128,160]{2,0,1:T(2,128)} %copy.138), calls=%async_computation | async-start | bytes 524288 | tf_op jit(solution)/shard_map/all_to_all | solution.py:132
  57.6 2.0 copy_bitcast_fusion
  59.5 6.2 %all-to-all-done = f32[2,128,160]{2,0,1:T(2,128)S(1)} async-done(((f32[2,128,160]{2,0,1:T(2,128)}), f32[2,128,160]{2,0,1:T(2,128)S(1)}, u32[]{:S(2)}, u32[]{:S(2)}) %all-to-all-start) | async-done | bytes 163872 | tf_op jit(solution)/shard_map/all_to_all | solution.py:132
  65.7 5.5 %all-to-all-start.1 = ((bf16[128,16,128]{2,0,1:T(8,128)(2,1)}), bf16[128,16,128]{2,0,1:T(8,128)(2,1)}, u32[]{:S(2)}, u32[]{:S(2)}) async-start(bf16[128,16,128]{2,0,1:T(8,128)(2,1)} %copy_bitcast_fusion), calls=%async_computation.1 | async-start | bytes 1048576 | tf_op jit(solution)/shard_map/all_to_all | solution.py:165
  74.3 2.0 bitcast_reduce_fusion
  83.3 1.9 collective-permute-start.2
  86.9 2.0 collective-permute-start.4
  91.1 1.7 collective-permute-start.6
  106.2 2.2 collective-permute-start.13
  111.4 2.3 %collective-permute-done.14 = bf16[2,8,2048]{2,1,0:T(8,128)(2,1)S(1)} collective-permute-done((bf16[2,8,2048]{2,1,0:T(8,128)(2,1)S(1)}, bf16[2,8,2048]{2,1,0:T(8,128)(2,1)S(1)}, u32[]{:S(2)}, u32[]{:S(2)}) %collective-permute-start.14) | collective-permute-done | bytes 65568 | tf_op jit(solution)/shard_map/ppermute | solution.py:25
  114.3 1.8 fusion.45
  116.9 21.3 %all-to-all-start.2 = ((f32[2,128,128]{2,0,1:T(2,128)}), f32[2,128,128]{2,0,1:T(2,128)S(1)}, u32[]{:S(2)}, u32[]{:S(2)}) async-start(f32[2,128,128]{2,0,1:T(2,128)} %copy.161), calls=%async_computation.2 | async-start | bytes 262144 | tf_op jit(solution)/shard_map/all_to_all | solution.py:169
  140.2 3.9 %all-to-all-done.2 = f32[2,128,128]{2,0,1:T(2,128)S(1)} async-done(((f32[2,128,128]{2,0,1:T(2,128)}), f32[2,128,128]{2,0,1:T(2,128)S(1)}, u32[]{:S(2)}, u32[]{:S(2)}) %all-to-all-start.2) | async-done | bytes 131104 | tf_op jit(solution)/shard_map/all_to_all | solution.py:169
  145.5 30.0 %all_to_all.62 = bf16[16,16,2048]{2,1,0:T(8,128)(2,1)S(1)} all-to-all(bf16[16,16,2048]{2,1,0:T(8,128)(2,1)S(1)} %bitcast.120), channel_id=1, replica_groups=mesh['groups'=2,'ep'=16] {'ep'}, dimensions={0} | all-to-all | bytes 2097152 | tf_op jit(solution)/shard_map/all_to_all | solution.py:191
  175.5 4.6 %fusion = f32[16,16,1536]{2,1,0:T(8,128)S(1)} fusion(bf16[16,16,2048]{2,1,0:T(8,128)(2,1)S(1)} %all_to_all.62, bf16[1,2048,1536]{2,1,0:T(8,128)(2,1)} %param.22), kind=kOutput, calls=%fused_computation.1 | convolution fusion | flops 1610612736 | bytes 8912896 | tf_op jit(solution)/shard_map/nsd,df->nsf/dot_general | solution.py:189
  180.1 2.1 fusion.4
  182.1 4.5 %all-to-all-start.4 = ((bf16[16,16,2048]{2,1,0:T(8,128)(2,1)}), bf16[16,16,2048]{2,1,0:T(8,128)(2,1)}, u32[]{:S(2)}, u32[]{:S(2)}) async-start(bf16[16,16,2048]{2,1,0:T(8,128)(2,1)} %fusion.4), calls=%async_computation.4 | async-start | bytes 2097152 | tf_op jit(solution)/shard_map/all_to_all | solution.py:200
  187.5 24.1 %all-to-all-done.4 = bf16[16,16,2048]{2,1,0:T(8,128)(2,1)} async-done(((bf16[16,16,2048]{2,1,0:T(8,128)(2,1)}), bf16[16,16,2048]{2,1,0:T(8,128)(2,1)}, u32[]{:S(2)}, u32[]{:S(2)}) %all-to-all-start.4) | async-done | bytes 1048608 | tf_op jit(solution)/shard_map/all_to_all | solution.py:200
  211.6 3.6 %gather_fusion = bf16[128,2048]{1,0:T(8,128)(2,1)} fusion(bf16[256,2048]{1,0:T(8,128)(2,1)} %bitcast.33, s32[1024]{0:T(1024)S(1)} %pad_clamp_fusion), kind=kCustom, calls=%fused_computation | custom fusion | bytes 1049088 | tf_op jit(solution)/shard_map/gather | solution.py:201
  (129 shorter events, 44.5 us)
Async XLA Ops:
  7.2 172.9 %copy-start = (bf16[1,768,2048]{2,1,0:T(8,128)(2,1)S(1)}, bf16[1,768,2048]{2,1,0:T(8,128)(2,1)}, u32[]{:S(2)}) copy-start(bf16[1,768,2048]{2,1,0:T(8,128)(2,1)} %param.23) | copy-start | bytes 9437188
  7.2 42.2 %all-gather.2.cloned.1.call-start = ((), (), s32[]{:S(2)}) async-start(), calls=%async_computation.5 | async-start | bytes 1114112 | tf_op jit(solution)/shard_map/all_gather | solution.py:128
  14.0 35.4 %copy-start.10 = (bf16[2048,16]{0,1:T(8,128)(2,1)S(1)}, bf16[2048,16]{0,1:T(8,128)(2,1)}, u32[]{:S(2)}) copy-start(bf16[2048,16]{0,1:T(8,128)(2,1)} %param.20) | copy-start | bytes 196612
  18.5 41.0 %copy-start.6 = (s32[128]{0:T(128)}, s32[128]{0:T(128)S(1)}, u32[]{:S(2)}) copy-start(s32[128]{0:T(128)S(1)} %reshape.243) | copy-start | bytes 1540
  52.1 13.6 %all-to-all-start = ((f32[2,128,160]{2,0,1:T(2,128)}), f32[2,128,160]{2,0,1:T(2,128)S(1)}, u32[]{:S(2)}, u32[]{:S(2)}) async-start(f32[2,128,160]{2,0,1:T(2,128)} %copy.138), calls=%async_computation | async-start | bytes 524288 | tf_op jit(solution)/shard_map/all_to_all | solution.py:132
  65.7 48.6 %all-to-all-start.1 = ((bf16[128,16,128]{2,0,1:T(8,128)(2,1)}), bf16[128,16,128]{2,0,1:T(8,128)(2,1)}, u32[]{:S(2)}, u32[]{:S(2)}) async-start(bf16[128,16,128]{2,0,1:T(8,128)(2,1)} %copy_bitcast_fusion), calls=%async_computation.1 | async-start | bytes 1048576 | tf_op jit(solution)/shard_map/all_to_all | solution.py:165
  80.0 3.2 %collective-permute-start = (bf16[2,8,2048]{2,1,0:T(8,128)(2,1)S(1)}, bf16[2,8,2048]{2,1,0:T(8,128)(2,1)S(1)}, u32[]{:S(2)}, u32[]{:S(2)}) collective-permute-start(bf16[2,8,2048]{2,1,0:T(8,128)(2,1)S(1)} %convert_element_type.89), channel_id=1, source_target_pairs={{0,1},{1,2},{2,3},{3,4},{4,5},{5,6},{6,7},{7,8},{8,9},{9,10},{10,1... | collective-permute-start | bytes 196616 | tf_op jit(solution)/shard_map/ppermute | solution.py:25
  81.5 4.1 %collective-permute-start.1 = (bf16[2,8,2048]{2,1,0:T(8,128)(2,1)S(1)}, bf16[2,8,2048]{2,1,0:T(8,128)(2,1)S(1)}, u32[]{:S(2)}, u32[]{:S(2)}) collective-permute-start(bf16[2,8,2048]{2,1,0:T(8,128)(2,1)S(1)} %convert_element_type.89), channel_id=1, source_target_pairs={{0,15},{1,0},{2,1},{3,2},{4,3},{5,4},{6,5},{7,6},{8,7},{9,8},{10,9... | collective-permute-start | bytes 196616 | tf_op jit(solution)/shard_map/ppermute | solution.py:32
  83.3 3.7 %collective-permute-start.2 = (bf16[2,8,2048]{2,1,0:T(8,128)(2,1)S(1)}, bf16[2,8,2048]{2,1,0:T(8,128)(2,1)S(1)}, u32[]{:S(2)}, u32[]{:S(2)}) collective-permute-start(bf16[2,8,2048]{2,1,0:T(8,128)(2,1)S(1)} %collective-permute-done), channel_id=1, source_target_pairs={{0,1},{1,2},{2,3},{3,4},{4,5},{5,6},{6,7},{7,8},{8,9},{9,10},{10,1... | collective-permute-start | bytes 196616 | tf_op jit(solution)/shard_map/ppermute | solution.py:25
  85.6 4.1 %collective-permute-start.3 = (bf16[2,8,2048]{2,1,0:T(8,128)(2,1)S(1)}, bf16[2,8,2048]{2,1,0:T(8,128)(2,1)S(1)}, u32[]{:S(2)}, u32[]{:S(2)}) collective-permute-start(bf16[2,8,2048]{2,1,0:T(8,128)(2,1)S(1)} %collective-permute-done.1), channel_id=1, source_target_pairs={{0,15},{1,0},{2,1},{3,2},{4,3},{5,4},{6,5},{7,6},{8,7},{9,8},{10,9... | collective-permute-start | bytes 196616 | tf_op jit(solution)/shard_map/ppermute | solution.py:32
  86.3 57.9 %copy-start.1 = (f32[2,8,2048]{2,1,0:T(8,128)S(1)}, f32[2,8,2048]{2,1,0:T(8,128)}, u32[]{:S(2)}) copy-start(f32[2,8,2048]{2,1,0:T(8,128)} %param.15) | copy-start | bytes 393220
  86.9 4.1 %collective-permute-start.4 = (bf16[2,8,2048]{2,1,0:T(8,128)(2,1)S(1)}, bf16[2,8,2048]{2,1,0:T(8,128)(2,1)S(1)}, u32[]{:S(2)}, u32[]{:S(2)}) collective-permute-start(bf16[2,8,2048]{2,1,0:T(8,128)(2,1)S(1)} %collective-permute-done.2), channel_id=1, source_target_pairs={{0,1},{1,2},{2,3},{3,4},{4,5},{5,6},{6,7},{7,8},{8,9},{9,10},{10,1... | collective-permute-start | bytes 196616 | tf_op jit(solution)/shard_map/ppermute | solution.py:25
  89.7 4.4 %collective-permute-start.5 = (bf16[2,8,2048]{2,1,0:T(8,128)(2,1)S(1)}, bf16[2,8,2048]{2,1,0:T(8,128)(2,1)S(1)}, u32[]{:S(2)}, u32[]{:S(2)}) collective-permute-start(bf16[2,8,2048]{2,1,0:T(8,128)(2,1)S(1)} %collective-permute-done.3), channel_id=1, source_target_pairs={{0,15},{1,0},{2,1},{3,2},{4,3},{5,4},{6,5},{7,6},{8,7},{9,8},{10,9... | collective-permute-start | bytes 196616 | tf_op jit(solution)/shard_map/ppermute | solution.py:32
  91.1 4.7 %collective-permute-start.6 = (bf16[2,8,2048]{2,1,0:T(8,128)(2,1)S(1)}, bf16[2,8,2048]{2,1,0:T(8,128)(2,1)S(1)}, u32[]{:S(2)}, u32[]{:S(2)}) collective-permute-start(bf16[2,8,2048]{2,1,0:T(8,128)(2,1)S(1)} %collective-permute-done.4), channel_id=1, source_target_pairs={{0,1},{1,2},{2,3},{3,4},{4,5},{5,6},{6,7},{7,8},{8,9},{9,10},{10,1... | collective-permute-start | bytes 196616 | tf_op jit(solution)/shard_map/ppermute | solution.py:25
  94.1 4.5 %collective-permute-start.7 = (bf16[2,8,2048]{2,1,0:T(8,128)(2,1)S(1)}, bf16[2,8,2048]{2,1,0:T(8,128)(2,1)S(1)}, u32[]{:S(2)}, u32[]{:S(2)}) collective-permute-start(bf16[2,8,2048]{2,1,0:T(8,128)(2,1)S(1)} %collective-permute-done.5), channel_id=1, source_target_pairs={{0,15},{1,0},{2,1},{3,2},{4,3},{5,4},{6,5},{7,6},{8,7},{9,8},{10,9... | collective-permute-start | bytes 196616 | tf_op jit(solution)/shard_map/ppermute | solution.py:32
  95.7 4.7 %collective-permute-start.8 = (bf16[2,8,2048]{2,1,0:T(8,128)(2,1)S(1)}, bf16[2,8,2048]{2,1,0:T(8,128)(2,1)S(1)}, u32[]{:S(2)}, u32[]{:S(2)}) collective-permute-start(bf16[2,8,2048]{2,1,0:T(8,128)(2,1)S(1)} %collective-permute-done.6), channel_id=1, source_target_pairs={{0,1},{1,2},{2,3},{3,4},{4,5},{5,6},{6,7},{7,8},{8,9},{9,10},{10,1... | collective-permute-start | bytes 196616 | tf_op jit(solution)/shard_map/ppermute | solution.py:25
  98.7 3.7 %collective-permute-start.9 = (bf16[2,8,2048]{2,1,0:T(8,128)(2,1)S(1)}, bf16[2,8,2048]{2,1,0:T(8,128)(2,1)S(1)}, u32[]{:S(2)}, u32[]{:S(2)}) collective-permute-start(bf16[2,8,2048]{2,1,0:T(8,128)(2,1)S(1)} %collective-permute-done.7), channel_id=1, source_target_pairs={{0,15},{1,0},{2,1},{3,2},{4,3},{5,4},{6,5},{7,6},{8,7},{9,8},{10,9... | collective-permute-start | bytes 196616 | tf_op jit(solution)/shard_map/ppermute | solution.py:32
  100.5 4.6 %collective-permute-start.10 = (bf16[2,8,2048]{2,1,0:T(8,128)(2,1)S(1)}, bf16[2,8,2048]{2,1,0:T(8,128)(2,1)S(1)}, u32[]{:S(2)}, u32[]{:S(2)}) collective-permute-start(bf16[2,8,2048]{2,1,0:T(8,128)(2,1)S(1)} %collective-permute-done.8), channel_id=1, source_target_pairs={{0,1},{1,2},{2,3},{3,4},{4,5},{5,6},{6,7},{7,8},{8,9},{9,10},{10,1... | collective-permute-start | bytes 196616 | tf_op jit(solution)/shard_map/ppermute | solution.py:25
  102.4 3.8 %collective-permute-start.11 = (bf16[2,8,2048]{2,1,0:T(8,128)(2,1)S(1)}, bf16[2,8,2048]{2,1,0:T(8,128)(2,1)S(1)}, u32[]{:S(2)}, u32[]{:S(2)}) collective-permute-start(bf16[2,8,2048]{2,1,0:T(8,128)(2,1)S(1)} %collective-permute-done.9), channel_id=1, source_target_pairs={{0,15},{1,0},{2,1},{3,2},{4,3},{5,4},{6,5},{7,6},{8,7},{9,8},{10,9... | collective-permute-start | bytes 196616 | tf_op jit(solution)/shard_map/ppermute | solution.py:32
  105.0 4.6 %collective-permute-start.12 = (bf16[2,8,2048]{2,1,0:T(8,128)(2,1)S(1)}, bf16[2,8,2048]{2,1,0:T(8,128)(2,1)S(1)}, u32[]{:S(2)}, u32[]{:S(2)}) collective-permute-start(bf16[2,8,2048]{2,1,0:T(8,128)(2,1)S(1)} %collective-permute-done.10), channel_id=1, source_target_pairs={{0,1},{1,2},{2,3},{3,4},{4,5},{5,6},{6,7},{7,8},{8,9},{9,10},{10,1... | collective-permute-start | bytes 196616 | tf_op jit(solution)/shard_map/ppermute | solution.py:25
  106.2 4.6 %collective-permute-start.13 = (bf16[2,8,2048]{2,1,0:T(8,128)(2,1)S(1)}, bf16[2,8,2048]{2,1,0:T(8,128)(2,1)S(1)}, u32[]{:S(2)}, u32[]{:S(2)}) collective-permute-start(bf16[2,8,2048]{2,1,0:T(8,128)(2,1)S(1)} %collective-permute-done.11), channel_id=1, source_target_pairs={{0,15},{1,0},{2,1},{3,2},{4,3},{5,4},{6,5},{7,6},{8,7},{9,8},{10,9... | collective-permute-start | bytes 196616 | tf_op jit(solution)/shard_map/ppermute | solution.py:32
  109.6 4.1 %collective-permute-start.14 = (bf16[2,8,2048]{2,1,0:T(8,128)(2,1)S(1)}, bf16[2,8,2048]{2,1,0:T(8,128)(2,1)S(1)}, u32[]{:S(2)}, u32[]{:S(2)}) collective-permute-start(bf16[2,8,2048]{2,1,0:T(8,128)(2,1)S(1)} %collective-permute-done.12), channel_id=1, source_target_pairs={{0,1},{1,2},{2,3},{3,4},{4,5},{5,6},{6,7},{7,8},{8,9},{9,10},{10,1... | collective-permute-start | bytes 196616 | tf_op jit(solution)/shard_map/ppermute | solution.py:25
  116.9 27.3 %all-to-all-start.2 = ((f32[2,128,128]{2,0,1:T(2,128)}), f32[2,128,128]{2,0,1:T(2,128)S(1)}, u32[]{:S(2)}, u32[]{:S(2)}) async-start(f32[2,128,128]{2,0,1:T(2,128)} %copy.161), calls=%async_computation.2 | async-start | bytes 262144 | tf_op jit(solution)/shard_map/all_to_all | solution.py:169
  182.1 29.5 %all-to-all-start.4 = ((bf16[16,16,2048]{2,1,0:T(8,128)(2,1)}), bf16[16,16,2048]{2,1,0:T(8,128)(2,1)}, u32[]{:S(2)}, u32[]{:S(2)}) async-start(bf16[16,16,2048]{2,1,0:T(8,128)(2,1)} %fusion.4), calls=%async_computation.4 | async-start | bytes 2097152 | tf_op jit(solution)/shard_map/all_to_all | solution.py:200
  (8 other events, 27.3 us)
Sparse Core Ops, SparseCore 0:
  10.8 38.5 all-gather.1
